TPU v7x, 32 devices: a whole 2x2x4 slice. The times are simulated.
32 devices in a mesh: section: 4 (over x, core), seq: 8 (over z, y).
Axes of the slice: x: 2, y: 2, z: 4, core: 2. Of those that a mesh axis runs over, the one named last changes fastest.
Arguments:
- hidden: bfloat16 [2, 1024, 2688], P(None, 'seq'), may hold values from -6 to 6
- lengths: int32 [2], replicated, may hold values from 512 to 1024, as said below
- reward_pos: int32 [2], replicated, may hold values from 384 to 1023, as said below
- in_gain: bfloat16 [2688], P('seq'), may hold values from 0.099609375 to 1.8984375
- w_query: bfloat16 [2688, 2048], P('seq', 'section'), may hold values from -0.077151675 to 0.077151675
- w_key: bfloat16 [2688, 1024], P('seq', 'section'), may hold values from -0.077151675 to 0.077151675
- w_value: bfloat16 [2688, 1024], P('seq', 'section'), may hold values from -0.125 to 0.125
- query_gain: float32 [128], replicated, may hold values from 0.6 to 7
- key_gain: float32 [128], replicated, may hold values from 0.6 to 7
- w_out: bfloat16 [2048, 2688], P('section', 'seq'), may hold values from -0.125 to 0.125
- post_gain: bfloat16 [2688], P('seq'), may hold values from 0.099609375 to 1.8984375
- final_gain: bfloat16 [2688], P('seq'), may hold values from 0.099609375 to 1.8984375
- value_head: bfloat16 [2688], P('seq'), may hold values from -0.125 to 0.125
Outputs:
- token_values: float32 [2, 1024], P(None, 'seq')
- reward: float32 [2], replicated
Inputs may be any that keep to these rules, and one draw needn't show every extreme that they name: `lengths`: in every draw at least one micro-batch has all 1024 tokens valid. reward_pos[m] lies among the last 128 valid tokens of micro-batch m.
All inputs are finite; a program needn't handle non-finite values.
Results may differ from a plain program's by a relative error of at most 0.01.
Values may be sent and summed in bfloat16 or wider, within the bound.
A program may use at most 64 MiB of HBM per device.

v0:
```python
import jax
import jax.numpy as jnp
from jax import lax
from jax.sharding import PartitionSpec as P

HD = 128
GROUP = 2
WINDOW = 1024
norm_eps = 1e-06
query_scale = 168.0 ** (-0.5)
rope_base = 10000.0


def passed_along(array, axis, by):
    devices = lax.axis_size(axis)
    pairs = [(i, i + by) for i in range(devices) if 0 <= i + by < devices]
    return lax.ppermute(array, axis, pairs)


def rms_scale(values, gain_vec):
    return (
        values * lax.rsqrt(jnp.mean(values * values, axis=-1, keepdims=True) + norm_eps) * gain_vec
    )


def rotate_pairs(head_rows, positions):
    half_width = head_rows.shape[-1] // 2
    frequency = rope_base ** (
        -jnp.arange(half_width, dtype=jnp.float32) * 2.0 / head_rows.shape[-1]
    )
    angles = positions.astype(jnp.float32)[:, None] * frequency[None, :]
    target = (angles.shape[0],) + (1,) * (head_rows.ndim - 2) + (half_width,)
    cosine = jnp.cos(angles).reshape(target)
    sine_part = jnp.sin(angles).reshape(target)
    front_half = head_rows[..., :half_width]
    back_half = head_rows[..., half_width:]
    return jnp.concatenate(
        [front_half * cosine - back_half * sine_part, back_half * cosine + front_half * sine_part],
        axis=-1,
    )


def window_blocks(packed, tok_dev):
    block_count = WINDOW // tok_dev + 1
    blocks_held = [packed]
    for offset in range(1, block_count):
        blocks_held.append(passed_along(packed, "seq", offset))
    return jnp.concatenate(blocks_held[::-1], axis=1)


def window_attention(queries, keys_all, values_all, query_pos, key_pos):
    scores = jnp.einsum("qhgd,khd->hgqk", queries, keys_all, preferred_element_type=jnp.float32)
    allowed = (
        (key_pos[None, :] <= query_pos[:, None])
        & (key_pos[None, :] > query_pos[:, None] - WINDOW)
        & (key_pos[None, :] >= 0)
    )
    scores = jnp.where(allowed[None, None], scores, -1e30)
    row_top = jnp.max(scores, axis=-1, keepdims=True)
    exponent = jnp.exp(scores - row_top)
    attn_weights = (exponent / jnp.sum(exponent, axis=-1, keepdims=True)).astype(jnp.bfloat16)
    mixed_heads = jnp.einsum(
        "hgqk,khd->qhgd", attn_weights, values_all, preferred_element_type=jnp.float32
    )
    return mixed_heads.astype(jnp.bfloat16)


def local(
    hidden,
    lengths,
    reward_pos,
    in_gain,
    w_query,
    w_key,
    w_value,
    query_gain,
    key_gain,
    w_out,
    post_gain,
    final_gain,
    value_head,
):
    micro_count, tok_dev, width = hidden.shape
    row_count = micro_count * tok_dev
    qwidth = w_query.shape[1]
    kwidth = w_key.shape[1]
    heads_here = kwidth // HD
    widened = hidden.reshape(row_count, width).astype(jnp.float32)
    inverse = lax.rsqrt(jnp.mean(widened * widened, axis=-1, keepdims=True) + norm_eps)
    seq_pos = lax.axis_index("seq") * tok_dev + jnp.arange(tok_dev, dtype=jnp.int32)
    positions = jnp.tile(seq_pos, micro_count)
    gain_piece = lax.all_gather(in_gain, "seq", axis=0, tiled=True)
    query_piece = lax.all_gather(w_query, "seq", axis=0, tiled=True)
    key_piece = lax.all_gather(w_key, "seq", axis=0, tiled=True)
    value_piece = lax.all_gather(w_value, "seq", axis=0, tiled=True)
    post_piece = lax.all_gather(post_gain, "seq", axis=0, tiled=True)
    final_piece = lax.all_gather(final_gain, "seq", axis=0, tiled=True)
    head_piece = lax.all_gather(value_head, "seq", axis=0, tiled=True)
    normed = (widened * inverse * gain_piece.astype(jnp.float32)).astype(jnp.bfloat16)
    query_acc = jnp.dot(normed, query_piece, preferred_element_type=jnp.float32)
    key_acc = jnp.dot(normed, key_piece, preferred_element_type=jnp.float32)
    value_acc = jnp.dot(normed, value_piece, preferred_element_type=jnp.float32)
    post_full = post_piece.astype(jnp.float32)
    final_full = final_piece.astype(jnp.float32)
    head_full = head_piece.astype(jnp.float32)
    folded = (query_acc, key_acc, value_acc, post_full, final_full, head_full)
    queries = folded[0].reshape(row_count, heads_here, GROUP, HD)
    queries = (rotate_pairs(rms_scale(queries, query_gain), positions) * query_scale).astype(
        jnp.bfloat16
    )
    keys_new = folded[1].reshape(row_count, heads_here, HD)
    keys_new = (
        rotate_pairs(rms_scale(keys_new, key_gain), positions)
        .astype(jnp.bfloat16)
        .reshape(row_count, kwidth)
    )
    vals_new = folded[2].astype(jnp.bfloat16)
    packed = jnp.concatenate([keys_new, vals_new], axis=1).reshape(micro_count, tok_dev, 2 * kwidth)
    window_rows = window_blocks(packed, tok_dev)
    key_pos = seq_pos[0] - WINDOW + jnp.arange(WINDOW + tok_dev, dtype=jnp.int32)
    mixed_list = []
    for micro_id in range(micro_count):
        block_queries = queries[micro_id * tok_dev : (micro_id + 1) * tok_dev]
        keys_all = window_rows[micro_id, :, :kwidth].reshape(-1, heads_here, HD)
        values_all = window_rows[micro_id, :, kwidth:].reshape(-1, heads_here, HD)
        mixed_list.append(
            window_attention(block_queries, keys_all, values_all, seq_pos, key_pos).reshape(
                tok_dev, qwidth
            )
        )
    mixed_all = jnp.concatenate(mixed_list, axis=0)
    branch = jnp.dot(
        mixed_all,
        lax.all_gather(w_out, "seq", axis=1, tiled=True),
        preferred_element_type=jnp.float32,
    )
    post_full, final_full, head_full = (folded[3], folded[4], folded[5])
    share_width = width // lax.axis_size("section")
    offset = lax.axis_index("section") * share_width
    share = lax.psum_scatter(branch, "section", scatter_dimension=1, tiled=True)
    branch_sq = lax.psum(jnp.sum(share * share, axis=1), "section")
    share_scale = lax.rsqrt(branch_sq / width + norm_eps)[:, None]
    post_share = lax.dynamic_slice_in_dim(post_full, offset, share_width, 0)
    updated = (
        lax.dynamic_slice_in_dim(widened, offset, share_width, 1) + share * share_scale * post_share
    ).astype(jnp.bfloat16)
    updated_wide = updated.astype(jnp.float32)
    residual_sq = lax.psum(jnp.sum(updated_wide * updated_wide, axis=1), "section")
    final_share = lax.dynamic_slice_in_dim(final_full, offset, share_width, 0)
    last_rows = (
        updated_wide * lax.rsqrt(residual_sq / width + norm_eps)[:, None] * final_share
    ).astype(jnp.bfloat16)
    head_share = lax.dynamic_slice_in_dim(head_full, offset, share_width, 0).astype(jnp.bfloat16)
    raw_values = lax.psum(
        jnp.dot(last_rows, head_share, preferred_element_type=jnp.float32), "section"
    )
    raw_values = raw_values.reshape(micro_count, tok_dev)
    token_values = jnp.where(seq_pos[None, :] < lengths[:, None], raw_values, 0.0)
    partial_value = jnp.sum(
        jnp.where(seq_pos[None, :] == reward_pos[:, None], token_values, 0.0), axis=1
    )
    reward = lax.psum(partial_value, "seq")
    return (token_values, reward)


def solution(mesh):
    placed = (
        P(None, "seq", None),
        P(),
        P(),
        P("seq"),
        P("seq", "section"),
        P("seq", "section"),
        P("seq", "section"),
        P(),
        P(),
        P("section", "seq"),
        P("seq"),
        P("seq"),
        P("seq"),
    )
    return jax.shard_map(
        local, mesh=mesh, in_specs=placed, out_specs=(P(None, "seq"), P()), check_vma=False
    )
```

profile of v0, /device:TPU:0, one launch (start us, length us, event | category | flops | bytes accessed | tf_op | source)
XLA Modules:
  0.0 331.5 jit_solution(10913897586998984354)
XLA Ops:
  7.9 0.7 all-gather.7.cloned.1.call-update
  8.7 0.7 all-gather.9.cloned.1.call-update
  10.1 1.2 dynamic-slice
  12.0 0.9 dynamic-update-slice
  12.9 0.9 dynamic-update-slice.1
  13.8 0.9 dynamic-update-slice.2
  14.7 0.9 dynamic-update-slice.3
  15.5 39.5 %all-reduce.4 = (bf16[2688]{0:T(1024)(128)(2,1)S(1)}, bf16[2688]{0:T(1024)(128)(2,1)S(1)}, bf16[2688]{0:T(1024)(128)(2,1)S(1)}, bf16[2688]{0:T(1024)(128)(2,1)S(1)}) all-reduce(bf16[2688]{0:T(1024)(128)(2,1)S(1)} %dynamic-update-slice.3, bf16[2688]{0:T(1024)(128)(2,1)S(1)} %dynamic-update-slice, ...), channel_id=1, replica_groups=mesh['section'=4,'seq'=8] {'seq'}, use_global_device_ids=true, to_apply=%add.3 | all-reduce | flops 10752 | bytes 43008
  55.1 1.7 multiply_reduce_fusion
  56.8 1.7 copy.43
  58.4 2.9 multiply_convert_fusion.1
  61.7 2.6 copy.24
  64.3 2.4 multiply_reduce_fusion.3
  66.9 31.5 %all-gather.7.cloned.1.call-done = bf16[2688,256]{1,0:T(8,128)(2,1)} async-done(((bf16[336,256]{1,0:T(8,128)(2,1)}), bf16[2688,256]{1,0:T(8,128)(2,1)}) %all-gather.7.cloned.1.call-update) | async-done | bytes 1376272 | tf_op jit(solution)/shard_map/all_gather | solution.py:95
  98.4 2.4 fusion.15
  101.6 4.0 %collective-permute-start.1 = (bf16[2,128,512]{1,2,0:T(8,128)(2,1)S(1)}, bf16[2,128,512]{1,2,0:T(8,128)(2,1)S(1)}, u32[]{:S(2)}, u32[]{:S(2)}) collective-permute-start(bf16[2,128,512]{1,2,0:T(8,128)(2,1)S(1)} %pad_maximum_fusion), channel_id=1, source_target_pairs={{0,7},{8,15},{16,23},{24,31}} | collective-permute-start | bytes 786440 | tf_op jit(solution)/shard_map/ppermute | solution.py:17
  105.6 1.3 collective-permute-start.2
  106.9 1.5 and_and_fusion
  108.4 1.3 collective-permute-start.3
  109.7 1.3 collective-permute-start.4
  111.0 2.4 collective-permute-start.5
  113.6 2.9 collective-permute-done.1
  116.5 1.3 collective-permute-start.6
  117.8 9.9 %collective-permute-done.2 = bf16[2,128,512]{1,2,0:T(8,128)(2,1)S(1)} collective-permute-done((bf16[2,128,512]{1,2,0:T(8,128)(2,1)S(1)}, bf16[2,128,512]{1,2,0:T(8,128)(2,1)S(1)}, u32[]{:S(2)}, u32[]{:S(2)}) %collective-permute-start.2) | collective-permute-done | bytes 262176 | tf_op jit(solution)/shard_map/ppermute | solution.py:17
  127.7 1.5 collective-permute-start.7
  129.2 5.3 %collective-permute-done.3 = bf16[2,128,512]{1,2,0:T(8,128)(2,1)S(1)} collective-permute-done((bf16[2,128,512]{1,2,0:T(8,128)(2,1)S(1)}, bf16[2,128,512]{1,2,0:T(8,128)(2,1)S(1)}, u32[]{:S(2)}, u32[]{:S(2)}) %collective-permute-start.3) | collective-permute-done | bytes 262176 | tf_op jit(solution)/shard_map/ppermute | solution.py:17
  134.6 5.6 %collective-permute-done.4 = bf16[2,128,512]{1,2,0:T(8,128)(2,1)S(1)} collective-permute-done((bf16[2,128,512]{1,2,0:T(8,128)(2,1)S(1)}, bf16[2,128,512]{1,2,0:T(8,128)(2,1)S(1)}, u32[]{:S(2)}, u32[]{:S(2)}) %collective-permute-start.4) | collective-permute-done | bytes 262176 | tf_op jit(solution)/shard_map/ppermute | solution.py:17
  140.3 5.6 %collective-permute-done.5 = bf16[2,128,512]{1,2,0:T(8,128)(2,1)S(1)} collective-permute-done((bf16[2,128,512]{1,2,0:T(8,128)(2,1)S(1)}, bf16[2,128,512]{1,2,0:T(8,128)(2,1)S(1)}, u32[]{:S(2)}, u32[]{:S(2)}) %collective-permute-start.5) | collective-permute-done | bytes 262176 | tf_op jit(solution)/shard_map/ppermute | solution.py:17
  145.9 3.4 %collective-permute-done.6 = bf16[2,128,512]{1,2,0:T(8,128)(2,1)S(1)} collective-permute-done((bf16[2,128,512]{1,2,0:T(8,128)(2,1)S(1)}, bf16[2,128,512]{1,2,0:T(8,128)(2,1)S(1)}, u32[]{:S(2)}, u32[]{:S(2)}) %collective-permute-start.6) | collective-permute-done | bytes 262176 | tf_op jit(solution)/shard_map/ppermute | solution.py:17
  149.5 1.2 fusion.60
  150.8 27.7 %all-gather.9.cloned.1.call-done = bf16[2688,512]{1,0:T(8,128)(2,1)} async-done(((bf16[336,512]{1,0:T(8,128)(2,1)}), bf16[2688,512]{1,0:T(8,128)(2,1)}) %all-gather.9.cloned.1.call-update) | async-done | bytes 2752528 | tf_op jit(solution)/shard_map/all_gather | solution.py:93
  178.5 4.5 %copy.27 = bf16[512,2688]{1,0:T(8,128)(2,1)} copy(bf16[512,2688]{0,1:T(8,128)(2,1)} %bitcast.94) | data formatting | bytes 5505024 | tf_op jit(solution)/shard_map/dot_general | solution.py:100
  183.0 3.2 multiply_reduce_fusion.2
  186.4 0.8 fusion.19
  187.1 2.1 fusion.64
  189.2 1.8 fusion.61
  191.1 3.2 fusion.14
  194.3 3.1 fusion.13
  197.3 46.1 %all-gather.11.cloned.1.call-done = bf16[512,2688]{0,1:T(8,128)(2,1)} async-done(((bf16[512,336]{0,1:T(8,128)(2,1)}), bf16[512,2688]{0,1:T(8,128)(2,1)}) %all-gather.11.cloned.1.call-update) | async-done | bytes 2752528 | tf_op jit(solution)/shard_map/all_gather | solution.py:134
  243.4 4.3 %fusion.24 = f32[256,2688]{0,1:T(8,128)} fusion(bf16[512,2688]{0,1:T(8,128)(2,1)} %all-gather.11.cloned.1.call-done, bf16[128,512]{0,1:T(8,128)(2,1)} %bitcast.108, bf16[128,512]{0,1:T(8,128)(2,1)} %bitcast.107), kind=kOutput, calls=%fused_computation.39 | convolution fusion | flops 705167360 | bytes 5767168 | tf_op jit(solution)/shard_map/dot_general | solution.py:132
  248.0 33.8 %reduce-scatter.2.cloned.1.call-done = f32[256,672]{0,1:T(8,128)} async-done(((f32[256,2688]{0,1:T(8,128)}), f32[256,672]{0,1:T(8,128)}) %reduce-scatter.2.cloned.1.call-update) | async-done | bytes 688144 | tf_op jit(solution)/shard_map/reduce_scatter | solution.py:140
  281.8 1.2 multiply_reduce_fusion.1
  283.0 5.8 %psum.28 = f32[256]{0:T(256)S(1)} all-reduce(f32[256]{0:T(256)S(1)} %multiply_reduce_fusion.1), channel_id=1, replica_groups=mesh['section'=4,'seq'=8] {'section'}, use_global_device_ids=true, to_apply=%region_9.10 | all-reduce | flops 256 | bytes 2048 | tf_op jit(solution)/shard_map/psum | solution.py:141
  288.8 1.3 fusion.16
  290.1 5.7 %psum.29 = f32[256]{0:T(256)S(1)} all-reduce(f32[256]{0:T(256)S(1)} %get-tuple-element.8), channel_id=1, replica_groups=mesh['section'=4,'seq'=8] {'section'}, use_global_device_ids=true, to_apply=%region_11.12 | all-reduce | flops 256 | bytes 2048 | tf_op jit(solution)/shard_map/psum | solution.py:148
  296.0 6.3 %psum.30 = f32[2,128]{1,0:T(2,128)S(1)} all-reduce(f32[2,128]{1,0:T(2,128)S(1)} %bitcast.110), channel_id=1, replica_groups=mesh['section'=4,'seq'=8] {'section'}, use_global_device_ids=true, to_apply=%region_12.13 | all-reduce | flops 256 | bytes 2048 | tf_op jit(solution)/shard_map/psum | solution.py:154
  302.3 0.7 fusion.48
  303.1 21.9 %psum.31 = f32[2]{0:T(128)} all-reduce(f32[2]{0:T(128)S(1)} %get-tuple-element.6), channel_id=1, replica_groups=mesh['section'=4,'seq'=8] {'seq'}, use_global_device_ids=true, to_apply=%region_14.15 | all-reduce | flops 2 | bytes 16 | tf_op jit(solution)/shard_map/psum | solution.py:162
  (62 shorter events, 4.1 us)
Async XLA Ops:
  7.2 54.5 %all-gather.5.cloned.1.call-start = ((), (), s32[]{:S(2)}) async-start(), calls=%async_computation.1 | async-start | bytes 1548288 | tf_op jit(solution)/shard_map/all_gather | solution.py:94
  7.9 90.5 %all-gather.7.cloned.1.call-start = ((), (), s32[]{:S(2)}) async-start(), calls=%async_computation.2 | async-start | bytes 1548288 | tf_op jit(solution)/shard_map/all_gather | solution.py:95
  8.6 169.8 %all-gather.9.cloned.1.call-start = ((), (), s32[]{:S(2)}) async-start(), calls=%async_computation.3 | async-start | bytes 3096576 | tf_op jit(solution)/shard_map/all_gather | solution.py:93
  9.4 234.0 %all-gather.11.cloned.1.call-start = ((), (), s32[]{:S(2)}) async-start(), calls=%async_computation.4 | async-start | bytes 3096576 | tf_op jit(solution)/shard_map/all_gather | solution.py:134
  10.0 271.8 %reduce-scatter.2.cloned.1.call-start = ((), (), s32[]{:S(2)}) async-start(), calls=%async_computation.5 | async-start | bytes 3440640 | tf_op jit(solution)/shard_map/reduce_scatter | solution.py:140
  61.7 5.0 %copy-start.1 = (f32[128]{0:T(128)S(1)}, f32[128]{0:T(128)}, u32[]{:S(2)}) copy-start(f32[128]{0:T(128)} %param.21) | copy-start | bytes 1540
  100.9 10.1 %collective-permute-start = (bf16[2,128,512]{1,2,0:T(8,128)(2,1)S(1)}, bf16[2,128,512]{1,2,0:T(8,128)(2,1)S(1)}, u32[]{:S(2)}, u32[]{:S(2)}) collective-permute-start(bf16[2,128,512]{1,2,0:T(8,128)(2,1)S(1)} %pad_maximum_fusion), channel_id=1, source_target_pairs={} | collective-permute-start | bytes 786440 | tf_op jit(solution)/shard_map/ppermute | solution.py:17
  101.6 14.9 %collective-permute-start.1 = (bf16[2,128,512]{1,2,0:T(8,128)(2,1)S(1)}, bf16[2,128,512]{1,2,0:T(8,128)(2,1)S(1)}, u32[]{:S(2)}, u32[]{:S(2)}) collective-permute-start(bf16[2,128,512]{1,2,0:T(8,128)(2,1)S(1)} %pad_maximum_fusion), channel_id=1, source_target_pairs={{0,7},{8,15},{16,23},{24,31}} | collective-permute-start | bytes 786440 | tf_op jit(solution)/shard_map/ppermute | solution.py:17
  105.6 22.1 %collective-permute-start.2 = (bf16[2,128,512]{1,2,0:T(8,128)(2,1)S(1)}, bf16[2,128,512]{1,2,0:T(8,128)(2,1)S(1)}, u32[]{:S(2)}, u32[]{:S(2)}) collective-permute-start(bf16[2,128,512]{1,2,0:T(8,128)(2,1)S(1)} %pad_maximum_fusion), channel_id=1, source_target_pairs={{0,6},{1,7},{8,14},{9,15},{16,22},{17,23},{24,30},{25,31}} | collective-permute-start | bytes 786440 | tf_op jit(solution)/shard_map/ppermute | solution.py:17
  108.4 26.2 %collective-permute-start.3 = (bf16[2,128,512]{1,2,0:T(8,128)(2,1)S(1)}, bf16[2,128,512]{1,2,0:T(8,128)(2,1)S(1)}, u32[]{:S(2)}, u32[]{:S(2)}) collective-permute-start(bf16[2,128,512]{1,2,0:T(8,128)(2,1)S(1)} %pad_maximum_fusion), channel_id=1, source_target_pairs={{0,5},{1,6},{2,7},{8,13},{9,14},{10,15},{16,21},{17,22},{18,23},{2... | collective-permute-start | bytes 786440 | tf_op jit(solution)/shard_map/ppermute | solution.py:17
  109.7 30.5 %collective-permute-start.4 = (bf16[2,128,512]{1,2,0:T(8,128)(2,1)S(1)}, bf16[2,128,512]{1,2,0:T(8,128)(2,1)S(1)}, u32[]{:S(2)}, u32[]{:S(2)}) collective-permute-start(bf16[2,128,512]{1,2,0:T(8,128)(2,1)S(1)} %pad_maximum_fusion), channel_id=1, source_target_pairs={{0,4},{1,5},{2,6},{3,7},{8,12},{9,13},{10,14},{11,15},{16,20},{17,... | collective-permute-start | bytes 786440 | tf_op jit(solution)/shard_map/ppermute | solution.py:17
  111.0 34.8 %collective-permute-start.5 = (bf16[2,128,512]{1,2,0:T(8,128)(2,1)S(1)}, bf16[2,128,512]{1,2,0:T(8,128)(2,1)S(1)}, u32[]{:S(2)}, u32[]{:S(2)}) collective-permute-start(bf16[2,128,512]{1,2,0:T(8,128)(2,1)S(1)} %pad_maximum_fusion), channel_id=1, source_target_pairs={{0,3},{1,4},{2,5},{3,6},{4,7},{8,11},{9,12},{10,13},{11,14},{12,15... | collective-permute-start | bytes 786440 | tf_op jit(solution)/shard_map/ppermute | solution.py:17
  116.5 32.9 %collective-permute-start.6 = (bf16[2,128,512]{1,2,0:T(8,128)(2,1)S(1)}, bf16[2,128,512]{1,2,0:T(8,128)(2,1)S(1)}, u32[]{:S(2)}, u32[]{:S(2)}) collective-permute-start(bf16[2,128,512]{1,2,0:T(8,128)(2,1)S(1)} %pad_maximum_fusion), channel_id=1, source_target_pairs={{0,2},{1,3},{2,4},{3,5},{4,6},{5,7},{8,10},{9,11},{10,12},{11,13},... | collective-permute-start | bytes 786440 | tf_op jit(solution)/shard_map/ppermute | solution.py:17
  127.7 21.7 %collective-permute-start.7 = (bf16[2,128,512]{1,2,0:T(8,128)(2,1)S(1)}, bf16[2,128,512]{1,2,0:T(8,128)(2,1)S(1)}, u32[]{:S(2)}, u32[]{:S(2)}) collective-permute-start(bf16[2,128,512]{1,2,0:T(8,128)(2,1)S(1)} %pad_maximum_fusion), channel_id=1, source_target_pairs={{0,1},{1,2},{2,3},{3,4},{4,5},{5,6},{6,7},{8,9},{9,10},{10,11},{11... | collective-permute-start | bytes 786440 | tf_op jit(solution)/shard_map/ppermute | solution.py:17
  183.0 3.2 copy-start.2
  186.4 2.9 copy-start
  247.7 54.6 %copy-start.3 = (s32[2]{0:T(128)S(1)}, s32[2]{0:T(128)}, u32[]{:S(2)}) copy-start(s32[2]{0:T(128)} %param.15) | copy-start | bytes 28
  247.7 54.6 %copy-start.4 = (s32[2]{0:T(128)S(1)}, s32[2]{0:T(128)}, u32[]{:S(2)}) copy-start(s32[2]{0:T(128)} %param.14) | copy-start | bytes 28
Sparse Core Ops, SparseCore 0:
  10.2 45.0 all-gather.4
  57.4 40.9 all-gather.6
  100.6 77.8 all-gather.8
  180.5 62.8 all-gather.10
  247.9 33.8 reduce-scatter.1
where the time goes:
time: 332 us; the launch traced here: 331 us
  waiting for transfers between devices  174 us (52%)
  blocking collectives  79.1 us (24%)
  matrix products  22.7 us (7%)
  local copies, waits for them, and re-layouts  15.4 us (5%)
  between operations  14.8 us (4%)
  starting transfers between devices  14 us (4%)
  other arithmetic  11.1 us (3%)
    all_gather x1, waiting for transfers between devices, local(): lax.all_gather(w_out, 'seq', axis=1, tiled=True)  46.1 us
    unnamed x1, blocking collectives  39.5 us
    reduce_scatter x1, waiting for transfers between devices, local(): share = lax.psum_scatter(branch, 'section', scatter_dimension=1, tiled=True)  33.8 us
    ppermute x8, waiting for transfers between devices, passed_along(): return lax.ppermute(array, axis, pairs)  32.7 us
    all_gather x1, waiting for transfers between devices, local(): value_piece = lax.all_gather(w_value, 'seq', axis=0, tiled=True)  31.5 us
    all_gather x1, waiting for transfers between devices, local(): query_piece = lax.all_gather(w_query, 'seq', axis=0, tiled=True)  27.7 us
    psum x1, blocking collectives, local(): reward = lax.psum(partial_value, 'seq')  21.9 us
    ppermute x8, starting transfers between devices, passed_along(): return lax.ppermute(array, axis, pairs)  13.8 us
  transfers between devices with their start and end apart: 13, of which 10 were waited for; matrix products, arithmetic and copies ran while one was open for 12% of the time, Pallas kernels for 0%

commit v1 on v0

--- a/solution.py
+++ b/solution.py
@@ -131,7 +131,7 @@
     mixed_all = jnp.concatenate(mixed_list, axis=0)
     branch = jnp.dot(
         mixed_all,
-        lax.all_gather(w_out, "seq", axis=1, tiled=True),
+        jnp.concatenate(lax.all_gather(w_out, axis_name="seq"), axis=1),
         preferred_element_type=jnp.float32,
     )
     post_full, final_full, head_full = (folded[3], folded[4], folded[5])

time: 332 us -> 343 us (1.033)
  waiting for transfers between devices: 174 us -> 185 us
  matrix products: 22.7 us -> 18.2 us
  local copies, waits for them, and re-layouts: 15.4 us -> 18.9 us
    all_gather x1, waiting for transfers between devices: 46.1 us -> 58.2 us  [local(): lax.all_gather(w_out, axis_name='seq')]
    unnamed x27 -> x34, local copies, waits for them, and re-layouts: 5.26 us -> 9.06 us
  transfers between devices with their start and end apart: 13 -> 13, of which waited for: 10 -> 10; matrix products, arithmetic and copies ran while one was open for 12% -> 9% of each run, Pallas kernels for 0% -> 0%
where the time goes in v1:
time: 343 us; the launch traced here: 342 us
  waiting for transfers between devices  185 us (54%)
  blocking collectives  79.1 us (23%)
  local copies, waits for them, and re-layouts  18.9 us (6%)
  matrix products  18.2 us (5%)
  between operations  14.9 us (4%)
  starting transfers between devices  14 us (4%)
  other arithmetic  11.6 us (3%)
    all_gather x1, waiting for transfers between devices, local(): lax.all_gather(w_out, axis_name='seq')  58.2 us
    unnamed x1, blocking collectives  39.5 us
    reduce_scatter x1, waiting for transfers between devices, local(): share = lax.psum_scatter(branch, 'section', scatter_dimension=1, tiled=True)  33.4 us
    ppermute x8, waiting for transfers between devices, passed_along(): return lax.ppermute(array, axis, pairs)  32.7 us
    all_gather x1, waiting for transfers between devices, local(): value_piece = lax.all_gather(w_value, 'seq', axis=0, tiled=True)  30.5 us
    all_gather x1, waiting for transfers between devices, local(): query_piece = lax.all_gather(w_query, 'seq', axis=0, tiled=True)  27.7 us
    psum x1, blocking collectives, local(): reward = lax.psum(partial_value, 'seq')  21.9 us
    ppermute x8, starting transfers between devices, passed_along(): return lax.ppermute(array, axis, pairs)  13.8 us
  transfers between devices with their start and end apart: 13, of which 10 were waited for; matrix products, arithmetic and copies ran while one was open for 9% of the time, Pallas kernels for 0%

profile of v1, /device:TPU:0, one launch (start us, length us, event | category | flops | bytes accessed | tf_op | source)
XLA Modules:
  0.0 341.8 jit_solution(16684824448332908040)
XLA Ops:
  10.1 1.2 dynamic-slice
  12.0 0.9 dynamic-update-slice
  12.9 0.9 dynamic-update-slice.1
  13.8 0.9 dynamic-update-slice.2
  14.7 0.9 dynamic-update-slice.3
  15.5 39.5 %all-reduce.4 = (bf16[2688]{0:T(1024)(128)(2,1)S(1)}, bf16[2688]{0:T(1024)(128)(2,1)S(1)}, bf16[2688]{0:T(1024)(128)(2,1)S(1)}, bf16[2688]{0:T(1024)(128)(2,1)S(1)}) all-reduce(bf16[2688]{0:T(1024)(128)(2,1)S(1)} %dynamic-update-slice.3, bf16[2688]{0:T(1024)(128)(2,1)S(1)} %dynamic-update-slice, ...), channel_id=1, replica_groups=mesh['section'=4,'seq'=8] {'seq'}, use_global_device_ids=true, to_apply=%add.3 | all-reduce | flops 10752 | bytes 43008
  55.1 1.7 multiply_reduce_fusion
  56.8 1.7 copy.55
  58.4 3.9 %multiply_convert_fusion.1 = bf16[2,128,2688]{2,1,0:T(8,128)(2,1)} fusion(bf16[2,128,2688]{2,1,0:T(8,128)(2,1)} %param.13, f32[2688]{0:T(1024)S(1)} %convert_element_type.89, f32[2,128]{1,0:T(2,128)S(1)} %get-tuple-element.20), kind=kLoop, calls=%fused_computation.11 | loop fusion | flops 2752512 | bytes 2764288 | tf_op jit(solution)/shard_map/convert_element_type | solution.py:99
  62.7 2.6 copy.35
  65.3 2.3 multiply_reduce_fusion.3
  67.9 30.5 %all-gather.8.cloned.1.call-done = bf16[2688,256]{1,0:T(8,128)(2,1)} async-done(((bf16[336,256]{1,0:T(8,128)(2,1)}), bf16[2688,256]{1,0:T(8,128)(2,1)}) %all-gather.8.cloned.1.call-update) | async-done | bytes 1376272 | tf_op jit(solution)/shard_map/all_gather | solution.py:95
  98.4 2.4 fusion.15
  101.6 4.0 %collective-permute-start.1 = (bf16[2,128,512]{1,2,0:T(8,128)(2,1)S(1)}, bf16[2,128,512]{1,2,0:T(8,128)(2,1)S(1)}, u32[]{:S(2)}, u32[]{:S(2)}) collective-permute-start(bf16[2,128,512]{1,2,0:T(8,128)(2,1)S(1)} %pad_maximum_fusion), channel_id=1, source_target_pairs={{0,7},{8,15},{16,23},{24,31}} | collective-permute-start | bytes 786440 | tf_op jit(solution)/shard_map/ppermute | solution.py:17
  105.6 1.3 collective-permute-start.2
  106.9 1.5 and_and_fusion
  108.4 1.3 collective-permute-start.3
  109.7 1.3 collective-permute-start.4
  111.1 2.4 collective-permute-start.5
  113.6 2.9 collective-permute-done.1
  116.5 1.3 collective-permute-start.6
  117.8 9.9 %collective-permute-done.2 = bf16[2,128,512]{1,2,0:T(8,128)(2,1)S(1)} collective-permute-done((bf16[2,128,512]{1,2,0:T(8,128)(2,1)S(1)}, bf16[2,128,512]{1,2,0:T(8,128)(2,1)S(1)}, u32[]{:S(2)}, u32[]{:S(2)}) %collective-permute-start.2) | collective-permute-done | bytes 262176 | tf_op jit(solution)/shard_map/ppermute | solution.py:17
  127.7 1.5 collective-permute-start.7
  129.3 5.3 %collective-permute-done.3 = bf16[2,128,512]{1,2,0:T(8,128)(2,1)S(1)} collective-permute-done((bf16[2,128,512]{1,2,0:T(8,128)(2,1)S(1)}, bf16[2,128,512]{1,2,0:T(8,128)(2,1)S(1)}, u32[]{:S(2)}, u32[]{:S(2)}) %collective-permute-start.3) | collective-permute-done | bytes 262176 | tf_op jit(solution)/shard_map/ppermute | solution.py:17
  134.7 5.6 %collective-permute-done.4 = bf16[2,128,512]{1,2,0:T(8,128)(2,1)S(1)} collective-permute-done((bf16[2,128,512]{1,2,0:T(8,128)(2,1)S(1)}, bf16[2,128,512]{1,2,0:T(8,128)(2,1)S(1)}, u32[]{:S(2)}, u32[]{:S(2)}) %collective-permute-start.4) | collective-permute-done | bytes 262176 | tf_op jit(solution)/shard_map/ppermute | solution.py:17
  140.3 5.6 %collective-permute-done.5 = bf16[2,128,512]{1,2,0:T(8,128)(2,1)S(1)} collective-permute-done((bf16[2,128,512]{1,2,0:T(8,128)(2,1)S(1)}, bf16[2,128,512]{1,2,0:T(8,128)(2,1)S(1)}, u32[]{:S(2)}, u32[]{:S(2)}) %collective-permute-start.5) | collective-permute-done | bytes 262176 | tf_op jit(solution)/shard_map/ppermute | solution.py:17
  145.9 3.4 %collective-permute-done.6 = bf16[2,128,512]{1,2,0:T(8,128)(2,1)S(1)} collective-permute-done((bf16[2,128,512]{1,2,0:T(8,128)(2,1)S(1)}, bf16[2,128,512]{1,2,0:T(8,128)(2,1)S(1)}, u32[]{:S(2)}, u32[]{:S(2)}) %collective-permute-start.6) | collective-permute-done | bytes 262176 | tf_op jit(solution)/shard_map/ppermute | solution.py:17
  149.6 1.2 fusion.60
  150.8 27.7 %all-gather.10.cloned.1.call-done = bf16[2688,512]{1,0:T(8,128)(2,1)} async-done(((bf16[336,512]{1,0:T(8,128)(2,1)}), bf16[2688,512]{1,0:T(8,128)(2,1)}) %all-gather.10.cloned.1.call-update) | async-done | bytes 2752528 | tf_op jit(solution)/shard_map/all_gather | solution.py:93
  178.5 3.3 copy.38
  181.8 2.3 multiply_reduce_fusion.2
  184.4 0.8 copy-done.1
  185.2 0.9 fusion.64
  186.1 0.9 fusion.61
  187.0 58.2 %all-gather.12.cloned.1.call-done = bf16[4096,336]{0,1:T(8,128)(2,1)} async-done(((bf16[512,336]{0,1:T(8,128)(2,1)}), bf16[4096,336]{0,1:T(8,128)(2,1)}) %all-gather.12.cloned.1.call-update) | async-done | bytes 2752528 | tf_op jit(solution)/shard_map/all_gather | solution.py:134
  245.2 3.0 copy.60
  248.2 0.9 copy.45
  249.2 2.6 fusion.14
  251.7 3.1 fusion.13
  254.8 3.3 fusion.24
  258.5 33.4 %reduce-scatter.2.cloned.1.call-done = f32[256,672]{0,1:T(8,128)} async-done(((f32[256,2688]{0,1:T(8,128)}), f32[256,672]{0,1:T(8,128)}) %reduce-scatter.2.cloned.1.call-update) | async-done | bytes 688144 | tf_op jit(solution)/shard_map/reduce_scatter | solution.py:140
  291.9 1.2 multiply_reduce_fusion.1
  293.1 5.8 %psum.28 = f32[256]{0:T(256)S(1)} all-reduce(f32[256]{0:T(256)S(1)} %multiply_reduce_fusion.1), channel_id=1, replica_groups=mesh['section'=4,'seq'=8] {'section'}, use_global_device_ids=true, to_apply=%region_9.10 | all-reduce | flops 256 | bytes 2048 | tf_op jit(solution)/shard_map/psum | solution.py:141
  298.9 1.5 fusion.16
  300.4 5.7 %psum.29 = f32[256]{0:T(256)S(1)} all-reduce(f32[256]{0:T(256)S(1)} %get-tuple-element.8), channel_id=1, replica_groups=mesh['section'=4,'seq'=8] {'section'}, use_global_device_ids=true, to_apply=%region_11.12 | all-reduce | flops 256 | bytes 2048 | tf_op jit(solution)/shard_map/psum | solution.py:148
  306.3 6.3 %psum.30 = f32[2,128]{1,0:T(2,128)S(1)} all-reduce(f32[2,128]{1,0:T(2,128)S(1)} %bitcast.120), channel_id=1, replica_groups=mesh['section'=4,'seq'=8] {'section'}, use_global_device_ids=true, to_apply=%region_12.13 | all-reduce | flops 256 | bytes 2048 | tf_op jit(solution)/shard_map/psum | solution.py:154
  312.6 0.7 fusion.48
  313.4 21.9 %psum.31 = f32[2]{0:T(128)} all-reduce(f32[2]{0:T(128)S(1)} %get-tuple-element.6), channel_id=1, replica_groups=mesh['section'=4,'seq'=8] {'seq'}, use_global_device_ids=true, to_apply=%region_14.15 | all-reduce | flops 2 | bytes 16 | tf_op jit(solution)/shard_map/psum | solution.py:162
  (70 shorter events, 5.6 us)
Async XLA Ops:
  7.2 55.5 %all-gather.6.cloned.1.call-start = ((), (), s32[]{:S(2)}) async-start(), calls=%async_computation.1 | async-start | bytes 1548288 | tf_op jit(solution)/shard_map/all_gather | solution.py:94
  7.9 90.5 %all-gather.8.cloned.1.call-start = ((), (), s32[]{:S(2)}) async-start(), calls=%async_computation.2 | async-start | bytes 1548288 | tf_op jit(solution)/shard_map/all_gather | solution.py:95
  8.6 169.8 %all-gather.10.cloned.1.call-start = ((), (), s32[]{:S(2)}) async-start(), calls=%async_computation.3 | async-start | bytes 3096576 | tf_op jit(solution)/shard_map/all_gather | solution.py:93
  9.4 235.9 %all-gather.12.cloned.1.call-start = ((), (), s32[]{:S(2)}) async-start(), calls=%async_computation.5 | async-start | bytes 3096576 | tf_op jit(solution)/shard_map/all_gather | solution.py:134
  10.0 281.9 %reduce-scatter.2.cloned.1.call-start = ((), (), s32[]{:S(2)}) async-start(), calls=%async_computation.4 | async-start | bytes 3440640 | tf_op jit(solution)/shard_map/reduce_scatter | solution.py:140
  58.4 39.9 %copy-start = (f32[256,2688]{0,1:T(8,128)}, f32[256,2688]{0,1:T(8,128)S(1)}, u32[]{:S(2)}) copy-start(f32[256,2688]{0,1:T(8,128)S(1)} %copy.55) | copy-start | bytes 8257540
  62.7 5.0 %copy-start.4 = (f32[128]{0:T(128)S(1)}, f32[128]{0:T(128)}, u32[]{:S(2)}) copy-start(f32[128]{0:T(128)} %param.21) | copy-start | bytes 1540
  100.9 10.1 %collective-permute-start = (bf16[2,128,512]{1,2,0:T(8,128)(2,1)S(1)}, bf16[2,128,512]{1,2,0:T(8,128)(2,1)S(1)}, u32[]{:S(2)}, u32[]{:S(2)}) collective-permute-start(bf16[2,128,512]{1,2,0:T(8,128)(2,1)S(1)} %pad_maximum_fusion), channel_id=1, source_target_pairs={} | collective-permute-start | bytes 786440 | tf_op jit(solution)/shard_map/ppermute | solution.py:17
  101.6 14.9 %collective-permute-start.1 = (bf16[2,128,512]{1,2,0:T(8,128)(2,1)S(1)}, bf16[2,128,512]{1,2,0:T(8,128)(2,1)S(1)}, u32[]{:S(2)}, u32[]{:S(2)}) collective-permute-start(bf16[2,128,512]{1,2,0:T(8,128)(2,1)S(1)} %pad_maximum_fusion), channel_id=1, source_target_pairs={{0,7},{8,15},{16,23},{24,31}} | collective-permute-start | bytes 786440 | tf_op jit(solution)/shard_map/ppermute | solution.py:17
  105.6 22.1 %collective-permute-start.2 = (bf16[2,128,512]{1,2,0:T(8,128)(2,1)S(1)}, bf16[2,128,512]{1,2,0:T(8,128)(2,1)S(1)}, u32[]{:S(2)}, u32[]{:S(2)}) collective-permute-start(bf16[2,128,512]{1,2,0:T(8,128)(2,1)S(1)} %pad_maximum_fusion), channel_id=1, source_target_pairs={{0,6},{1,7},{8,14},{9,15},{16,22},{17,23},{24,30},{25,31}} | collective-permute-start | bytes 786440 | tf_op jit(solution)/shard_map/ppermute | solution.py:17
  108.4 26.2 %collective-permute-start.3 = (bf16[2,128,512]{1,2,0:T(8,128)(2,1)S(1)}, bf16[2,128,512]{1,2,0:T(8,128)(2,1)S(1)}, u32[]{:S(2)}, u32[]{:S(2)}) collective-permute-start(bf16[2,128,512]{1,2,0:T(8,128)(2,1)S(1)} %pad_maximum_fusion), channel_id=1, source_target_pairs={{0,5},{1,6},{2,7},{8,13},{9,14},{10,15},{16,21},{17,22},{18,23},{2... | collective-permute-start | bytes 786440 | tf_op jit(solution)/shard_map/ppermute | solution.py:17
  109.7 30.5 %collective-permute-start.4 = (bf16[2,128,512]{1,2,0:T(8,128)(2,1)S(1)}, bf16[2,128,512]{1,2,0:T(8,128)(2,1)S(1)}, u32[]{:S(2)}, u32[]{:S(2)}) collective-permute-start(bf16[2,128,512]{1,2,0:T(8,128)(2,1)S(1)} %pad_maximum_fusion), channel_id=1, source_target_pairs={{0,4},{1,5},{2,6},{3,7},{8,12},{9,13},{10,14},{11,15},{16,20},{17,... | collective-permute-start | bytes 786440 | tf_op jit(solution)/shard_map/ppermute | solution.py:17
  111.1 34.8 %collective-permute-start.5 = (bf16[2,128,512]{1,2,0:T(8,128)(2,1)S(1)}, bf16[2,128,512]{1,2,0:T(8,128)(2,1)S(1)}, u32[]{:S(2)}, u32[]{:S(2)}) collective-permute-start(bf16[2,128,512]{1,2,0:T(8,128)(2,1)S(1)} %pad_maximum_fusion), channel_id=1, source_target_pairs={{0,3},{1,4},{2,5},{3,6},{4,7},{8,11},{9,12},{10,13},{11,14},{12,15... | collective-permute-start | bytes 786440 | tf_op jit(solution)/shard_map/ppermute | solution.py:17
  116.5 32.9 %collective-permute-start.6 = (bf16[2,128,512]{1,2,0:T(8,128)(2,1)S(1)}, bf16[2,128,512]{1,2,0:T(8,128)(2,1)S(1)}, u32[]{:S(2)}, u32[]{:S(2)}) collective-permute-start(bf16[2,128,512]{1,2,0:T(8,128)(2,1)S(1)} %pad_maximum_fusion), channel_id=1, source_target_pairs={{0,2},{1,3},{2,4},{3,5},{4,6},{5,7},{8,10},{9,11},{10,12},{11,13},... | collective-permute-start | bytes 786440 | tf_op jit(solution)/shard_map/ppermute | solution.py:17
  127.7 21.7 %collective-permute-start.7 = (bf16[2,128,512]{1,2,0:T(8,128)(2,1)S(1)}, bf16[2,128,512]{1,2,0:T(8,128)(2,1)S(1)}, u32[]{:S(2)}, u32[]{:S(2)}) collective-permute-start(bf16[2,128,512]{1,2,0:T(8,128)(2,1)S(1)} %pad_maximum_fusion), channel_id=1, source_target_pairs={{0,1},{1,2},{2,3},{3,4},{4,5},{5,6},{6,7},{8,9},{9,10},{10,11},{11... | collective-permute-start | bytes 786440 | tf_op jit(solution)/shard_map/ppermute | solution.py:17
  181.8 2.4 copy-start.5
  184.1 1.1 copy-start.1
  184.1 1.1 copy-start.3
  184.4 2.7 copy-start.2
  258.2 54.4 %copy-start.6 = (s32[2]{0:T(128)S(1)}, s32[2]{0:T(128)}, u32[]{:S(2)}) copy-start(s32[2]{0:T(128)} %param.15) | copy-start | bytes 28
  258.2 54.4 %copy-start.7 = (s32[2]{0:T(128)S(1)}, s32[2]{0:T(128)}, u32[]{:S(2)}) copy-start(s32[2]{0:T(128)} %param.14) | copy-start | bytes 28
Sparse Core Ops, SparseCore 0:
  10.2 45.0 all-gather.5
  57.4 40.9 all-gather.7
  100.6 77.8 all-gather.9
  180.4 64.8 all-gather.11
  258.3 33.5 reduce-scatter.1
